TPU v7x, 128 devices: a whole 4x4x4 slice. The times are simulated.
128 devices in a mesh: gx: 8 (over x, core), gy: 4 (over y), gz: 4 (over z).
Axes of the slice: x: 4, y: 4, z: 4, core: 2. Of those that a mesh axis runs over, the one named last changes fastest.
Arguments:
- start_block: float32 [16, 32, 64, 512], P(None, 'gx', 'gy', 'gz')
- basis: bfloat16 [256, 32, 64, 512], P(None, 'gx', 'gy', 'gz')
- trans_x: float32 [32, 64, 512], P('gx', 'gy', 'gz'), may hold values from 0.05 to 1
- trans_y: float32 [32, 64, 512], P('gx', 'gy', 'gz'), may hold values from 0.05 to 1
- trans_z: float32 [32, 64, 512], P('gx', 'gy', 'gz'), may hold values from 0.05 to 1
- pore_volume: float32 [32, 64, 512], P('gx', 'gy', 'gz'), may hold values from 0.5 to 2
- shift_table: float32 [16], replicated, may hold values from 0.5 to 4
- shift_index: int32 [1], replicated, may hold values from 0 to 15
- fault_send: int32 [128, 128, 32], P(('gx', 'gy', 'gz')), may hold values from 0 to 8191
- fault_recv: int32 [128, 128, 32], P(('gx', 'gy', 'gz')), may hold values from 0 to 8191
- fault_trans: float32 [128, 128, 32], P(('gx', 'gy', 'gz')), may hold values from 0.05 to 0.5
- well_cells: int32 [64], replicated, may hold values from 0 to 1048575
Outputs:
- new_block: float32 [16, 32, 64, 512], P(None, 'gx', 'gy', 'gz')
- first_coeffs: float32 [256, 16], replicated
- coeffs: float32 [256, 16], replicated
- well_resp: float32 [64, 16], replicated
Inputs may be any that keep to these rules, and one draw needn't show every extreme that they name: fault_send[d, p, s] is a local cell number on device d; the value of that cell feeds a connection into device p. fault_recv[d, p, s] is a local cell number on device d. `well_cells`: flat cell index, last dimension fastest.
All inputs are finite; a program needn't handle non-finite values.
Results may differ from a plain program's by a relative error of at most 0.0065.
Values sent between devices are 32-bit elements; how exact they have to be, the bound alone decides.
A program may use at most 128 MiB of HBM per device.

v0:
```python
import math
import jax
import jax.numpy as jnp
from jax import lax
from jax.sharding import PartitionSpec as P

TERMS = 8


def from_behind(value, axis, by):
    size = lax.axis_size(axis)
    pairs = [(i, i + by) for i in range(size) if 0 <= i + by < size]
    return lax.ppermute(value, axis, pairs)


def extended(value, sides, width):
    for axis, dim in sides:
        size, length = (lax.axis_size(axis), value.shape[dim])
        up = [(i, (i + 1) % size) for i in range(size - 1)]
        down = [(j, i) for i, j in up]
        last = lax.slice_in_dim(value, length - width, length, axis=dim)
        initial = lax.slice_in_dim(value, 0, width, axis=dim)
        before = lax.ppermute(last, axis, up)
        after = lax.ppermute(initial, axis, down)
        value = jnp.concatenate([before, value, after], axis=dim)
    return value


def local(
    start_block,
    basis,
    trans_x,
    trans_y,
    trans_z,
    pore_volume,
    shift_table,
    shift_index,
    fault_send,
    fault_recv,
    fault_trans,
    well_cells,
):
    columns, size_x, size_y, size_z = start_block.shape
    cells = size_x * size_y * size_z
    count_x = lax.axis_size("gx")
    count_y = lax.axis_size("gy")
    count_z = lax.axis_size("gz")
    index_x = lax.axis_index("gx")
    index_y = lax.axis_index("gy")
    index_z = lax.axis_index("gz")
    full_x = size_x * count_x
    full_y = size_y * count_y
    full_z = size_z * count_z
    shape3 = (size_x, size_y, size_z)
    pos_x = lax.broadcasted_iota(jnp.int32, shape3, 0) + index_x * size_x
    pos_y = lax.broadcasted_iota(jnp.int32, shape3, 1) + index_y * size_y
    pos_z = lax.broadcasted_iota(jnp.int32, shape3, 2) + index_z * size_z
    upper_x = jnp.where(pos_x < full_x - 1, trans_x, 0.0)
    upper_y = jnp.where(pos_y < full_y - 1, trans_y, 0.0)
    upper_z = jnp.where(pos_z < full_z - 1, trans_z, 0.0)
    edge_x = from_behind(upper_x[-1:, :, :], "gx", 1)
    edge_y = from_behind(upper_y[:, -1:, :], "gy", 1)
    edge_z = from_behind(upper_z[:, :, -1:], "gz", 1)
    lower_x = jnp.concatenate([edge_x, upper_x[:-1, :, :]], axis=0)
    lower_y = jnp.concatenate([edge_y, upper_y[:, :-1, :]], axis=1)
    lower_z = jnp.concatenate([edge_z, upper_z[:, :, :-1]], axis=2)
    shift = jnp.sum(
        jnp.where(
            jnp.arange(shift_table.shape[0], dtype=jnp.int32) == shift_index[0], shift_table, 0.0
        )
    )
    send_flat = fault_send[0].reshape(-1)
    recv_flat = fault_recv[0].reshape(-1)
    weight_flat = fault_trans[0].reshape(-1)
    fault_diag = jnp.zeros((cells,), jnp.float32).at[recv_flat].add(weight_flat).reshape(shape3)
    diagonal = (
        upper_x + lower_x + upper_y + lower_y + upper_z + lower_z + shift * pore_volume + fault_diag
    )
    sigma = 1.0 / 0.9
    weight_now = 1.0 / sigma
    solution = jnp.zeros_like(start_block)
    residual = start_block
    direction = residual / diagonal
    for number in range(TERMS):
        solution = solution + direction
        if number < TERMS - 1:
            grown = extended(direction, (("gx", 1), ("gy", 2), ("gz", 3)), 1)
            operate_flat = direction.reshape(columns, cells)
            incoming = lax.all_to_all(
                operate_flat[:, send_flat],
                ("gx", "gy", "gz"),
                split_axis=1,
                concat_axis=1,
                tiled=True,
            )
            beside = upper_x * grown[:, 2:, 1:-1, 1:-1] + lower_x * grown[:, :-2, 1:-1, 1:-1]
            beside = (
                beside + upper_y * grown[:, 1:-1, 2:, 1:-1] + lower_y * grown[:, 1:-1, :-2, 1:-1]
            )
            beside = (
                beside + upper_z * grown[:, 1:-1, 1:-1, 2:] + lower_z * grown[:, 1:-1, 1:-1, :-2]
            )
            remote = (
                jnp.zeros((columns, cells), jnp.float32)
                .at[:, recv_flat]
                .add(weight_flat * incoming)
            )
            residual = residual - (diagonal * direction - beside - remote.reshape(direction.shape))
            weight_new = 1.0 / (2.0 * sigma - weight_now)
            direction = weight_new * weight_now * direction + 2.0 * weight_new / 0.9 * (
                residual / diagonal
            )
            weight_now = weight_new
    plane = full_y * full_z
    well_x = well_cells // plane
    well_y = well_cells // full_z % full_y
    well_z = well_cells % full_z
    owned = (
        (well_x // size_x == index_x)
        & (well_y // size_y == index_y)
        & (well_z // size_z == index_z)
    )
    local_cell = (well_x % size_x * size_y + well_y % size_y) * size_z + well_z % size_z
    flat_basis = basis.reshape(basis.shape[0], cells)
    flat_x = solution.reshape(columns, cells)
    first_term = jnp.dot(
        flat_basis, flat_x.astype(jnp.bfloat16).T, preferred_element_type=jnp.float32
    )
    first_coeffs = lax.psum(first_term, ("gx", "gy", "gz"))
    first_rest = flat_x - jnp.dot(
        first_coeffs.astype(jnp.bfloat16).T, flat_basis, preferred_element_type=jnp.float32
    )
    second_term = jnp.dot(
        flat_basis, first_rest.astype(jnp.bfloat16).T, preferred_element_type=jnp.float32
    )
    second_coeffs = lax.psum(second_term, ("gx", "gy", "gz"))
    rest = first_rest - jnp.dot(
        second_coeffs.astype(jnp.bfloat16).T, flat_basis, preferred_element_type=jnp.float32
    )
    gram_term = jnp.dot(rest, rest.T, precision=lax.Precision.HIGHEST)
    gram, wells_value = lax.psum(
        (gram_term, jnp.where(owned[None, :], rest[:, local_cell], 0.0)), ("gx", "gy", "gz")
    )
    lower = jnp.linalg.cholesky(gram)
    scale = math.sqrt(full_x * full_y * full_z)
    new_flat = lax.linalg.triangular_solve(lower, rest, left_side=True, lower=True) * scale
    well_resp = (
        lax.linalg.triangular_solve(lower, wells_value, left_side=True, lower=True) * scale
    ).T
    return (
        new_flat.reshape(start_block.shape),
        first_coeffs,
        first_coeffs + second_coeffs,
        well_resp,
    )


def solution(mesh):
    in_specs = (
        P(None, "gx", "gy", "gz"),
        P(None, "gx", "gy", "gz"),
        P("gx", "gy", "gz"),
        P("gx", "gy", "gz"),
        P("gx", "gy", "gz"),
        P("gx", "gy", "gz"),
        P(),
        P(),
        P(("gx", "gy", "gz"), None, None),
        P(("gx", "gy", "gz"), None, None),
        P(("gx", "gy", "gz"), None, None),
        P(),
    )
    out_specs = (P(None, "gx", "gy", "gz"), P(), P(), P())
    return jax.shard_map(local, mesh=mesh, in_specs=in_specs, out_specs=out_specs, check_vma=False)
```

profile of v0, /device:TPU:1, one launch (start us, length us, event | category | flops | bytes accessed | tf_op | source)
XLA Modules:
  0.0 1015.0 jit_solution(15570318955301733830)
XLA Ops:
  19.2 21.9 %scatter_custom_fusion = f32[8192]{0:T(1024)S(1)} fusion(s32[4096]{0:T(1024)S(1)} %bitcast.158, f32[4096]{0:T(1024)S(1)} %reshape.239, f32[]{:T(128)} %constant.173.clone.1), kind=kCustom, calls=%fused_computation.323 | custom fusion | flops 4096 | bytes 32772 | tf_op jit(solution)/shard_map/scatter-add | solution.py:75
  59.0 16.4 %gather_fusion = f32[4096,16]{1,0:T(8,128)} fusion(f32[16,8192]{0,1:T(8,128)} %bitcast.125, s32[4096]{0:T(1024)S(1)} %broadcast_clamp_fusion), kind=kCustom, calls=%fused_computation | custom fusion | bytes 540672 | tf_op jit(solution)/shard_map/gather | solution.py:90
  78.8 11.2 %all-to-all-start = ((f32[128,1,512]{2,1,0:T(1,128)}), f32[128,1,512]{2,1,0:T(1,128)S(1)}, u32[]{:S(2)}, u32[]{:S(2)}) async-start(f32[128,1,512]{2,1,0:T(1,128)} %reshape.317), calls=%async_computation | async-start | bytes 524288 | tf_op jit(solution)/shard_map/all_to_all | solution.py:89
  113.2 25.0 %scatter_custom_fusion.1 = f32[16,8192]{0,1:T(8,128)} fusion(s32[4096]{0:T(1024)} %bitcast.159, f32[4096,16]{1,0:T(8,128)} %copy.299, f32[]{:T(128)} %constant.173.clone.1), kind=kCustom, calls=%fused_computation.40 | custom fusion | flops 65536 | bytes 524800 | tf_op jit(solution)/shard_map/scatter-add | solution.py:106
  161.3 16.4 %gather_fusion.1 = f32[4096,16]{1,0:T(8,128)} fusion(f32[16,8192]{0,1:T(8,128)} %bitcast.126, s32[4096]{0:T(1024)S(1)} %broadcast_clamp_fusion), kind=kCustom, calls=%fused_computation.1 | custom fusion | bytes 540672 | tf_op jit(solution)/shard_map/gather | solution.py:90
  181.0 11.4 %all-to-all-start.1 = ((f32[128,1,512]{2,1,0:T(1,128)}), f32[128,1,512]{2,1,0:T(1,128)}, u32[]{:S(2)}, u32[]{:S(2)}) async-start(f32[128,1,512]{2,1,0:T(1,128)} %reshape.319), calls=%async_computation.1 | async-start | bytes 524288 | tf_op jit(solution)/shard_map/all_to_all | solution.py:89
  216.0 24.8 %scatter_custom_fusion.2 = f32[16,8192]{0,1:T(8,128)} fusion(s32[4096]{0:T(1024)} %bitcast.160, f32[4096,16]{1,0:T(8,128)} %copy.314, f32[]{:T(128)} %constant.173.clone.1), kind=kCustom, calls=%fused_computation.38 | custom fusion | flops 65536 | bytes 524800 | tf_op jit(solution)/shard_map/scatter-add | solution.py:106
  264.2 16.4 %gather_fusion.2 = f32[4096,16]{1,0:T(8,128)} fusion(f32[16,8192]{0,1:T(8,128)} %bitcast.127, s32[4096]{0:T(1024)S(1)} %broadcast_clamp_fusion), kind=kCustom, calls=%fused_computation.2 | custom fusion | bytes 540672 | tf_op jit(solution)/shard_map/gather | solution.py:90
  284.0 11.4 %all-to-all-start.2 = ((f32[128,1,512]{2,1,0:T(1,128)}), f32[128,1,512]{2,1,0:T(1,128)}, u32[]{:S(2)}, u32[]{:S(2)}) async-start(f32[128,1,512]{2,1,0:T(1,128)} %reshape.321), calls=%async_computation.2 | async-start | bytes 524288 | tf_op jit(solution)/shard_map/all_to_all | solution.py:89
  319.0 24.8 %scatter_custom_fusion.3 = f32[16,8192]{0,1:T(8,128)} fusion(s32[4096]{0:T(1024)} %bitcast.161, f32[4096,16]{1,0:T(8,128)} %copy.329, f32[]{:T(128)} %constant.173.clone.1), kind=kCustom, calls=%fused_computation.36 | custom fusion | flops 65536 | bytes 524800 | tf_op jit(solution)/shard_map/scatter-add | solution.py:106
  366.5 16.4 %gather_fusion.3 = f32[4096,16]{1,0:T(8,128)} fusion(f32[16,8192]{0,1:T(8,128)} %bitcast.128, s32[4096]{0:T(1024)S(1)} %broadcast_clamp_fusion), kind=kCustom, calls=%fused_computation.3 | custom fusion | bytes 540672 | tf_op jit(solution)/shard_map/gather | solution.py:90
  386.3 11.4 %all-to-all-start.3 = ((f32[128,1,512]{2,1,0:T(1,128)}), f32[128,1,512]{2,1,0:T(1,128)}, u32[]{:S(2)}, u32[]{:S(2)}) async-start(f32[128,1,512]{2,1,0:T(1,128)} %reshape.323), calls=%async_computation.3 | async-start | bytes 524288 | tf_op jit(solution)/shard_map/all_to_all | solution.py:89
  423.3 24.8 %scatter_custom_fusion.4 = f32[16,8192]{0,1:T(8,128)} fusion(s32[4096]{0:T(1024)} %bitcast.162, f32[4096,16]{1,0:T(8,128)} %copy.344, f32[]{:T(128)} %constant.173.clone.1), kind=kCustom, calls=%fused_computation.34 | custom fusion | flops 65536 | bytes 524800 | tf_op jit(solution)/shard_map/scatter-add | solution.py:106
  473.4 16.4 %gather_fusion.4 = f32[4096,16]{1,0:T(8,128)} fusion(f32[16,8192]{0,1:T(8,128)} %bitcast.129, s32[4096]{0:T(1024)S(1)} %broadcast_clamp_fusion), kind=kCustom, calls=%fused_computation.4 | custom fusion | bytes 540672 | tf_op jit(solution)/shard_map/gather | solution.py:90
  493.1 10.8 %all-to-all-start.4 = ((f32[128,1,512]{2,1,0:T(1,128)}), f32[128,1,512]{2,1,0:T(1,128)}, u32[]{:S(2)}, u32[]{:S(2)}) async-start(f32[128,1,512]{2,1,0:T(1,128)} %reshape.325), calls=%async_computation.4 | async-start | bytes 524288 | tf_op jit(solution)/shard_map/all_to_all | solution.py:89
  532.9 24.8 %scatter_custom_fusion.5 = f32[16,8192]{0,1:T(8,128)} fusion(s32[4096]{0:T(1024)} %bitcast.163, f32[4096,16]{1,0:T(8,128)} %copy.359, f32[]{:T(128)} %constant.173.clone.1), kind=kCustom, calls=%fused_computation.32 | custom fusion | flops 65536 | bytes 524800 | tf_op jit(solution)/shard_map/scatter-add | solution.py:106
  582.4 16.4 %gather_fusion.5 = f32[4096,16]{1,0:T(8,128)} fusion(f32[16,8192]{0,1:T(8,128)} %bitcast.130, s32[4096]{0:T(1024)S(1)} %broadcast_clamp_fusion), kind=kCustom, calls=%fused_computation.5 | custom fusion | bytes 540672 | tf_op jit(solution)/shard_map/gather | solution.py:90
  639.8 24.8 %scatter_custom_fusion.6 = f32[16,8192]{0,1:T(8,128)} fusion(s32[4096]{0:T(1024)} %bitcast.164, f32[4096,16]{1,0:T(8,128)} %copy.374, f32[]{:T(128)} %constant.173.clone.1), kind=kCustom, calls=%fused_computation.30 | custom fusion | flops 65536 | bytes 524800 | tf_op jit(solution)/shard_map/scatter-add | solution.py:106
  690.8 16.4 %gather_fusion.6 = f32[4096,16]{1,0:T(8,128)} fusion(f32[16,8192]{0,1:T(8,128)} %bitcast.124, s32[4096]{0:T(1024)S(1)} %broadcast_clamp_fusion), kind=kCustom, calls=%fused_computation.6 | custom fusion | bytes 540672 | tf_op jit(solution)/shard_map/gather | solution.py:90
  712.8 11.4 %all-to-all-start.6 = ((f32[128,1,512]{2,1,0:T(1,128)}), f32[128,1,512]{2,1,0:T(1,128)}, u32[]{:S(2)}, u32[]{:S(2)}) async-start(f32[128,1,512]{2,1,0:T(1,128)} %reshape.329), calls=%async_computation.6 | async-start | bytes 524288 | tf_op jit(solution)/shard_map/all_to_all | solution.py:89
  761.0 24.8 %scatter_custom_fusion.7 = f32[16,8192]{0,1:T(8,128)} fusion(s32[4096]{0:T(1024)} %bitcast.165, f32[4096,16]{1,0:T(8,128)} %copy.389, f32[]{:T(128)} %constant.173.clone.1), kind=kCustom, calls=%fused_computation.28 | custom fusion | flops 65536 | bytes 524800 | tf_op jit(solution)/shard_map/scatter-add | solution.py:106
  795.7 67.1 %psum.28 = f32[256,16]{0,1:T(8,128)S(1)} all-reduce(f32[256,16]{0,1:T(8,128)S(1)} %fusion.24), channel_id=1, replica_groups=mesh['gx'=8,'gy'=4,'gz'=4] {'gx','gy','gz'}, use_global_device_ids=true, to_apply=%region_9.10 | all-reduce | flops 4096 | bytes 32768 | tf_op jit(solution)/shard_map/psum | solution.py:129
  870.0 62.8 %psum.29 = f32[256,16]{0,1:T(8,128)S(1)} all-reduce(f32[256,16]{0,1:T(8,128)S(1)} %fusion.27), channel_id=1, replica_groups=mesh['gx'=8,'gy'=4,'gz'=4] {'gx','gy','gz'}, use_global_device_ids=true, to_apply=%region_10.11 | all-reduce | flops 4096 | bytes 32768 | tf_op jit(solution)/shard_map/psum | solution.py:136
  944.2 64.1 %all-reduce = (f32[16,16]{0,1:T(8,128)S(1)}, f32[16,64]{0,1:T(8,128)S(1)}) all-reduce(f32[16,16]{0,1:T(8,128)S(1)} %fusion.165, f32[16,64]{0,1:T(8,128)S(1)} %select_bitcast_fusion), channel_id=1, replica_groups=mesh['gx'=8,'gy'=4,'gz'=4] {'gx','gy','gz'}, use_global_device_ids=true, to_apply=%region_11.12 | all-reduce | flops 1280 | bytes 10240 | tf_op jit(solution)/shard_map/psum | solution.py:141
  (386 shorter events, 439.6 us)
Async XLA Ops:
  1.6 39.6 %collective-permute-start = (f32[1,16,128]{2,1,0:T(8,128)S(1)}, f32[1,16,128]{2,1,0:T(8,128)S(1)}, u32[]{:S(2)}, u32[]{:S(2)}) collective-permute-start(f32[1,16,128]{2,1,0:T(8,128)S(1)} %slice.432), channel_id=1, source_target_pairs={{0,16},{16,32},{32,48},{48,64},{64,80},{80,96},{96,112},{1,17},{17... | collective-permute-start | bytes 24584 | tf_op jit(solution)/shard_map/ppermute | solution.py:13
  6.9 34.3 %collective-permute-start.1 = (f32[4,1,128]{2,1,0:T(1,128)S(1)}, f32[4,1,128]{2,1,0:T(1,128)S(1)}, u32[]{:S(2)}, u32[]{:S(2)}) collective-permute-start(f32[4,1,128]{2,1,0:T(1,128)S(1)} %slice.434), channel_id=1, source_target_pairs={{0,4},{4,8},{8,12},{1,5},{5,9},{9,13},{2,6},{6,10},{10,14},{3,7},{... | collective-permute-start | bytes 6152 | tf_op jit(solution)/shard_map/ppermute | solution.py:13
  11.0 30.2 %collective-permute-start.2 = (f32[4,16,1]{2,1,0:T(8,128)S(1)}, f32[4,16,1]{2,1,0:T(8,128)S(1)}, u32[]{:S(2)}, u32[]{:S(2)}) collective-permute-start(f32[4,16,1]{2,1,0:T(8,128)S(1)} %slice.436), channel_id=1, source_target_pairs={{0,1},{1,2},{2,3},{4,5},{5,6},{6,7},{8,9},{9,10},{10,11},{12,13},{... | collective-permute-start | bytes 776 | tf_op jit(solution)/shard_map/ppermute | solution.py:13
  51.0 38.9 %collective-permute-start.5 = (f32[16,6,1,128]{3,0,2,1:T(8,128)S(1)}, f32[16,6,1,128]{3,0,2,1:T(8,128)S(1)}, u32[]{:S(2)}, u32[]{:S(2)}) collective-permute-start(f32[16,6,1,128]{3,0,2,1:T(8,128)S(1)} %copy.398), channel_id=1, source_target_pairs={{4,0},{8,4},{12,8},{5,1},{9,5},{13,9},{6,2},{10,6},{14,10},{7,3},{... | collective-permute-start | bytes 147464 | tf_op jit(solution)/shard_map/ppermute | solution.py:24
  52.3 37.7 %collective-permute-start.6 = (f32[16,6,1,128]{3,0,2,1:T(8,128)S(1)}, f32[16,6,1,128]{3,0,2,1:T(8,128)S(1)}, u32[]{:S(2)}, u32[]{:S(2)}) collective-permute-start(f32[16,6,1,128]{3,0,2,1:T(8,128)S(1)} %copy.399), channel_id=1, source_target_pairs={{0,4},{4,8},{8,12},{1,5},{5,9},{9,13},{2,6},{6,10},{10,14},{3,7},{... | collective-permute-start | bytes 147464 | tf_op jit(solution)/shard_map/ppermute | solution.py:23
  78.8 23.4 %all-to-all-start = ((f32[128,1,512]{2,1,0:T(1,128)}), f32[128,1,512]{2,1,0:T(1,128)S(1)}, u32[]{:S(2)}, u32[]{:S(2)}) async-start(f32[128,1,512]{2,1,0:T(1,128)} %reshape.317), calls=%async_computation | async-start | bytes 524288 | tf_op jit(solution)/shard_map/all_to_all | solution.py:89
  153.3 39.2 %collective-permute-start.11 = (f32[16,6,1,128]{3,0,2,1:T(8,128)S(1)}, f32[16,6,1,128]{3,0,2,1:T(8,128)S(1)}, u32[]{:S(2)}, u32[]{:S(2)}) collective-permute-start(f32[16,6,1,128]{3,0,2,1:T(8,128)S(1)} %copy.400), channel_id=1, source_target_pairs={{4,0},{8,4},{12,8},{5,1},{9,5},{13,9},{6,2},{10,6},{14,10},{7,3},{... | collective-permute-start | bytes 147464 | tf_op jit(solution)/shard_map/ppermute | solution.py:24
  154.6 37.9 %collective-permute-start.12 = (f32[16,6,1,128]{3,0,2,1:T(8,128)S(1)}, f32[16,6,1,128]{3,0,2,1:T(8,128)S(1)}, u32[]{:S(2)}, u32[]{:S(2)}) collective-permute-start(f32[16,6,1,128]{3,0,2,1:T(8,128)S(1)} %copy.401), channel_id=1, source_target_pairs={{0,4},{4,8},{8,12},{1,5},{5,9},{9,13},{2,6},{6,10},{10,14},{3,7},{... | collective-permute-start | bytes 147464 | tf_op jit(solution)/shard_map/ppermute | solution.py:23
  181.0 23.5 %all-to-all-start.1 = ((f32[128,1,512]{2,1,0:T(1,128)}), f32[128,1,512]{2,1,0:T(1,128)}, u32[]{:S(2)}, u32[]{:S(2)}) async-start(f32[128,1,512]{2,1,0:T(1,128)} %reshape.319), calls=%async_computation.1 | async-start | bytes 524288 | tf_op jit(solution)/shard_map/all_to_all | solution.py:89
  256.1 39.4 %collective-permute-start.17 = (f32[16,6,1,128]{3,0,2,1:T(8,128)S(1)}, f32[16,6,1,128]{3,0,2,1:T(8,128)S(1)}, u32[]{:S(2)}, u32[]{:S(2)}) collective-permute-start(f32[16,6,1,128]{3,0,2,1:T(8,128)S(1)} %copy.402), channel_id=1, source_target_pairs={{4,0},{8,4},{12,8},{5,1},{9,5},{13,9},{6,2},{10,6},{14,10},{7,3},{... | collective-permute-start | bytes 147464 | tf_op jit(solution)/shard_map/ppermute | solution.py:24
  257.6 37.9 %collective-permute-start.18 = (f32[16,6,1,128]{3,0,2,1:T(8,128)S(1)}, f32[16,6,1,128]{3,0,2,1:T(8,128)S(1)}, u32[]{:S(2)}, u32[]{:S(2)}) collective-permute-start(f32[16,6,1,128]{3,0,2,1:T(8,128)S(1)} %copy.403), channel_id=1, source_target_pairs={{0,4},{4,8},{8,12},{1,5},{5,9},{9,13},{2,6},{6,10},{10,14},{3,7},{... | collective-permute-start | bytes 147464 | tf_op jit(solution)/shard_map/ppermute | solution.py:23
  284.0 25.2 %all-to-all-start.2 = ((f32[128,1,512]{2,1,0:T(1,128)}), f32[128,1,512]{2,1,0:T(1,128)}, u32[]{:S(2)}, u32[]{:S(2)}) async-start(f32[128,1,512]{2,1,0:T(1,128)} %reshape.321), calls=%async_computation.2 | async-start | bytes 524288 | tf_op jit(solution)/shard_map/all_to_all | solution.py:89
  358.6 39.2 %collective-permute-start.23 = (f32[16,6,1,128]{3,0,2,1:T(8,128)S(1)}, f32[16,6,1,128]{3,0,2,1:T(8,128)S(1)}, u32[]{:S(2)}, u32[]{:S(2)}) collective-permute-start(f32[16,6,1,128]{3,0,2,1:T(8,128)S(1)} %copy.404), channel_id=1, source_target_pairs={{4,0},{8,4},{12,8},{5,1},{9,5},{13,9},{6,2},{10,6},{14,10},{7,3},{... | collective-permute-start | bytes 147464 | tf_op jit(solution)/shard_map/ppermute | solution.py:24
  359.9 37.9 %collective-permute-start.24 = (f32[16,6,1,128]{3,0,2,1:T(8,128)S(1)}, f32[16,6,1,128]{3,0,2,1:T(8,128)S(1)}, u32[]{:S(2)}, u32[]{:S(2)}) collective-permute-start(f32[16,6,1,128]{3,0,2,1:T(8,128)S(1)} %copy.405), channel_id=1, source_target_pairs={{0,4},{4,8},{8,12},{1,5},{5,9},{9,13},{2,6},{6,10},{10,14},{3,7},{... | collective-permute-start | bytes 147464 | tf_op jit(solution)/shard_map/ppermute | solution.py:23
  386.3 27.2 %all-to-all-start.3 = ((f32[128,1,512]{2,1,0:T(1,128)}), f32[128,1,512]{2,1,0:T(1,128)}, u32[]{:S(2)}, u32[]{:S(2)}) async-start(f32[128,1,512]{2,1,0:T(1,128)} %reshape.323), calls=%async_computation.3 | async-start | bytes 524288 | tf_op jit(solution)/shard_map/all_to_all | solution.py:89
  464.2 39.8 %collective-permute-start.29 = (f32[16,6,1,128]{3,0,2,1:T(8,128)}, f32[16,6,1,128]{3,0,2,1:T(8,128)}, u32[]{:S(2)}, u32[]{:S(2)}) collective-permute-start(f32[16,6,1,128]{3,0,2,1:T(8,128)} %copy.406), channel_id=1, source_target_pairs={{4,0},{8,4},{12,8},{5,1},{9,5},{13,9},{6,2},{10,6},{14,10},{7,3},{... | collective-permute-start | bytes 147464 | tf_op jit(solution)/shard_map/ppermute | solution.py:24
  466.1 38.7 %collective-permute-start.30 = (f32[16,6,1,128]{3,0,2,1:T(8,128)}, f32[16,6,1,128]{3,0,2,1:T(8,128)}, u32[]{:S(2)}, u32[]{:S(2)}) collective-permute-start(f32[16,6,1,128]{3,0,2,1:T(8,128)} %copy.407), channel_id=1, source_target_pairs={{0,4},{4,8},{8,12},{1,5},{5,9},{9,13},{2,6},{6,10},{10,14},{3,7},{... | collective-permute-start | bytes 147464 | tf_op jit(solution)/shard_map/ppermute | solution.py:23
  493.1 30.5 %all-to-all-start.4 = ((f32[128,1,512]{2,1,0:T(1,128)}), f32[128,1,512]{2,1,0:T(1,128)}, u32[]{:S(2)}, u32[]{:S(2)}) async-start(f32[128,1,512]{2,1,0:T(1,128)} %reshape.325), calls=%async_computation.4 | async-start | bytes 524288 | tf_op jit(solution)/shard_map/all_to_all | solution.py:89
  573.2 40.9 %collective-permute-start.35 = (f32[16,6,1,128]{3,0,2,1:T(8,128)}, f32[16,6,1,128]{3,0,2,1:T(8,128)S(1)}, u32[]{:S(2)}, u32[]{:S(2)}) collective-permute-start(f32[16,6,1,128]{3,0,2,1:T(8,128)} %copy.408), channel_id=1, source_target_pairs={{4,0},{8,4},{12,8},{5,1},{9,5},{13,9},{6,2},{10,6},{14,10},{7,3},{... | collective-permute-start | bytes 147464 | tf_op jit(solution)/shard_map/ppermute | solution.py:24
  575.1 39.1 %collective-permute-start.36 = (f32[16,6,1,128]{3,0,2,1:T(8,128)}, f32[16,6,1,128]{3,0,2,1:T(8,128)}, u32[]{:S(2)}, u32[]{:S(2)}) collective-permute-start(f32[16,6,1,128]{3,0,2,1:T(8,128)} %copy.409), channel_id=1, source_target_pairs={{0,4},{4,8},{8,12},{1,5},{5,9},{9,13},{2,6},{6,10},{10,14},{3,7},{... | collective-permute-start | bytes 147464 | tf_op jit(solution)/shard_map/ppermute | solution.py:23
  604.3 26.6 %all-to-all-start.5 = ((f32[128,1,512]{2,1,0:T(1,128)}), f32[128,1,512]{2,1,0:T(1,128)S(1)}, u32[]{:S(2)}, u32[]{:S(2)}) async-start(f32[128,1,512]{2,1,0:T(1,128)} %reshape.327), calls=%async_computation.5 | async-start | bytes 524288 | tf_op jit(solution)/shard_map/all_to_all | solution.py:89
  681.6 42.6 %collective-permute-start.41 = (f32[16,6,1,128]{3,0,2,1:T(8,128)}, f32[16,6,1,128]{3,0,2,1:T(8,128)}, u32[]{:S(2)}, u32[]{:S(2)}) collective-permute-start(f32[16,6,1,128]{3,0,2,1:T(8,128)} %copy.410), channel_id=1, source_target_pairs={{4,0},{8,4},{12,8},{5,1},{9,5},{13,9},{6,2},{10,6},{14,10},{7,3},{... | collective-permute-start | bytes 147464 | tf_op jit(solution)/shard_map/ppermute | solution.py:24
  683.5 41.6 %collective-permute-start.42 = (f32[16,6,1,128]{3,0,2,1:T(8,128)}, f32[16,6,1,128]{3,0,2,1:T(8,128)}, u32[]{:S(2)}, u32[]{:S(2)}) collective-permute-start(f32[16,6,1,128]{3,0,2,1:T(8,128)} %copy.411), channel_id=1, source_target_pairs={{0,4},{4,8},{8,12},{1,5},{5,9},{9,13},{2,6},{6,10},{10,14},{3,7},{... | collective-permute-start | bytes 147464 | tf_op jit(solution)/shard_map/ppermute | solution.py:23
  712.8 33.5 %all-to-all-start.6 = ((f32[128,1,512]{2,1,0:T(1,128)}), f32[128,1,512]{2,1,0:T(1,128)}, u32[]{:S(2)}, u32[]{:S(2)}) async-start(f32[128,1,512]{2,1,0:T(1,128)} %reshape.329), calls=%async_computation.6 | async-start | bytes 524288 | tf_op jit(solution)/shard_map/all_to_all | solution.py:89
  (69 other events, 875.3 us)
where the time goes:
time: 1030 us; the launch traced here: 1010 us
  local copies, waits for them, and re-layouts  314 us (30%)
  other arithmetic  251 us (24%)
  starting transfers between devices  209 us (20%)
  blocking collectives  194 us (19%)
  waiting for transfers between devices  28 us (3%)
  matrix products  16.4 us (2%)
    scatter-add x7, other arithmetic, local(): remote = jnp.zeros((columns, cells), jnp.float32).at[:, recv_flat].add(we...  174 us
    gather x7, local copies, waits for them, and re-layouts, local(): operate_flat[:, send_flat]  115 us
    all_to_all x7, starting transfers between devices, local(): lax.all_to_all(operate_flat[:, send_flat], ('gx', 'gy', 'gz'), split_axis...  77.5 us
    ppermute x21, starting transfers between devices, extended(): before = lax.ppermute(last, axis, up)  77 us
    psum x1, blocking collectives, local(): first_coeffs = lax.psum(first_term, ('gx', 'gy', 'gz'))  67.1 us
    psum x1, blocking collectives, local(): lax.psum((gram_term, jnp.where(owned[None, :], rest[:, local_cell], 0.0))...  64.1 us
    psum x1, blocking collectives, local(): second_coeffs = lax.psum(second_term, ('gx', 'gy', 'gz'))  62.8 us
    all_to_all x22, local copies, waits for them, and re-layouts, local(): lax.all_to_all(operate_flat[:, send_flat], ('gx', 'gy', 'gz'), split_axis...  47.2 us
  transfers between devices with their start and end apart: 52, of which 21 were waited for; matrix products, arithmetic and copies ran while one was open for 24% of the time, Pallas kernels for 0%

commit v1 on v0

--- a/solution.py
+++ b/solution.py
@@ -126,7 +126,8 @@
     first_term = jnp.dot(
         flat_basis, flat_x.astype(jnp.bfloat16).T, preferred_element_type=jnp.float32
     )
-    first_coeffs = lax.psum(first_term, ("gx", "gy", "gz"))
+    partial = lax.psum(first_term, "gx")
+    first_coeffs = lax.psum(partial, ("gy", "gz"))
     first_rest = flat_x - jnp.dot(
         first_coeffs.astype(jnp.bfloat16).T, flat_basis, preferred_element_type=jnp.float32
     )

time: 1030 us -> 1060 us (1.029)
  blocking collectives: 194 us -> 226 us
    psum x1 -> x2, blocking collectives: 67.1 us -> 84 us  [the longest x1 61.3 us: local(): first_coeffs = lax.psum(partial, ('gy', 'gz'))]
    psum x1, blocking collectives: 62.8 us -> 78.9 us  [local(): second_coeffs = lax.psum(second_term, ('gx', 'gy', 'gz'))]
where the time goes in v1:
time: 1060 us; the launch traced here: 1050 us
  local copies, waits for them, and re-layouts  314 us (30%)
  other arithmetic  251 us (24%)
  blocking collectives  226 us (21%)
  starting transfers between devices  209 us (20%)
  waiting for transfers between devices  28 us (3%)
  matrix products  16.4 us (2%)
    scatter-add x7, other arithmetic, local(): remote = jnp.zeros((columns, cells), jnp.float32).at[:, recv_flat].add(we...  174 us
    gather x7, local copies, waits for them, and re-layouts, local(): operate_flat[:, send_flat]  114 us
    psum x1, blocking collectives, local(): second_coeffs = lax.psum(second_term, ('gx', 'gy', 'gz'))  78.9 us
    all_to_all x7, starting transfers between devices, local(): lax.all_to_all(operate_flat[:, send_flat], ('gx', 'gy', 'gz'), split_axis...  77.5 us
    ppermute x21, starting transfers between devices, extended(): before = lax.ppermute(last, axis, up)  77.1 us
    psum x1, blocking collectives, local(): lax.psum((gram_term, jnp.where(owned[None, :], rest[:, local_cell], 0.0))...  62.8 us
    psum x1, blocking collectives, local(): first_coeffs = lax.psum(partial, ('gy', 'gz'))  61.3 us
    all_to_all x22, local copies, waits for them, and re-layouts, local(): lax.all_to_all(operate_flat[:, send_flat], ('gx', 'gy', 'gz'), split_axis...  47.3 us
  transfers between devices with their start and end apart: 52, of which 21 were waited for; matrix products, arithmetic and copies ran while one was open for 24% of the time, Pallas kernels for 0%

profile of v1, /device:TPU:1, one launch (start us, length us, event | category | flops | bytes accessed | tf_op | source)
XLA Modules:
  0.0 1046.3 jit_solution(379598529864744819)
XLA Ops:
  19.2 21.9 %scatter_custom_fusion = f32[8192]{0:T(1024)S(1)} fusion(s32[4096]{0:T(1024)S(1)} %bitcast.158, f32[4096]{0:T(1024)S(1)} %reshape.239, f32[]{:T(128)} %constant.173.clone.1), kind=kCustom, calls=%fused_computation.323 | custom fusion | flops 4096 | bytes 32772 | tf_op jit(solution)/shard_map/scatter-add | solution.py:75
  59.0 16.3 %gather_fusion = f32[4096,16]{1,0:T(8,128)} fusion(f32[16,8192]{0,1:T(8,128)} %bitcast.125, s32[4096]{0:T(1024)S(1)} %broadcast_clamp_fusion), kind=kCustom, calls=%fused_computation | custom fusion | bytes 540672 | tf_op jit(solution)/shard_map/gather | solution.py:90
  78.7 11.2 %all-to-all-start = ((f32[128,1,512]{2,1,0:T(1,128)}), f32[128,1,512]{2,1,0:T(1,128)S(1)}, u32[]{:S(2)}, u32[]{:S(2)}) async-start(f32[128,1,512]{2,1,0:T(1,128)} %reshape.317), calls=%async_computation | async-start | bytes 524288 | tf_op jit(solution)/shard_map/all_to_all | solution.py:89
  113.1 25.0 %scatter_custom_fusion.1 = f32[16,8192]{0,1:T(8,128)} fusion(s32[4096]{0:T(1024)} %bitcast.159, f32[4096,16]{1,0:T(8,128)} %copy.299, f32[]{:T(128)} %constant.173.clone.1), kind=kCustom, calls=%fused_computation.40 | custom fusion | flops 65536 | bytes 524800 | tf_op jit(solution)/shard_map/scatter-add | solution.py:106
  161.2 16.3 %gather_fusion.1 = f32[4096,16]{1,0:T(8,128)} fusion(f32[16,8192]{0,1:T(8,128)} %bitcast.126, s32[4096]{0:T(1024)S(1)} %broadcast_clamp_fusion), kind=kCustom, calls=%fused_computation.1 | custom fusion | bytes 540672 | tf_op jit(solution)/shard_map/gather | solution.py:90
  180.9 11.4 %all-to-all-start.1 = ((f32[128,1,512]{2,1,0:T(1,128)}), f32[128,1,512]{2,1,0:T(1,128)}, u32[]{:S(2)}, u32[]{:S(2)}) async-start(f32[128,1,512]{2,1,0:T(1,128)} %reshape.319), calls=%async_computation.1 | async-start | bytes 524288 | tf_op jit(solution)/shard_map/all_to_all | solution.py:89
  215.9 24.9 %scatter_custom_fusion.2 = f32[16,8192]{0,1:T(8,128)} fusion(s32[4096]{0:T(1024)} %bitcast.160, f32[4096,16]{1,0:T(8,128)} %copy.314, f32[]{:T(128)} %constant.173.clone.1), kind=kCustom, calls=%fused_computation.38 | custom fusion | flops 65536 | bytes 524800 | tf_op jit(solution)/shard_map/scatter-add | solution.py:106
  264.1 16.3 %gather_fusion.2 = f32[4096,16]{1,0:T(8,128)} fusion(f32[16,8192]{0,1:T(8,128)} %bitcast.127, s32[4096]{0:T(1024)S(1)} %broadcast_clamp_fusion), kind=kCustom, calls=%fused_computation.2 | custom fusion | bytes 540672 | tf_op jit(solution)/shard_map/gather | solution.py:90
  283.8 11.4 %all-to-all-start.2 = ((f32[128,1,512]{2,1,0:T(1,128)}), f32[128,1,512]{2,1,0:T(1,128)}, u32[]{:S(2)}, u32[]{:S(2)}) async-start(f32[128,1,512]{2,1,0:T(1,128)} %reshape.321), calls=%async_computation.2 | async-start | bytes 524288 | tf_op jit(solution)/shard_map/all_to_all | solution.py:89
  318.8 24.9 %scatter_custom_fusion.3 = f32[16,8192]{0,1:T(8,128)} fusion(s32[4096]{0:T(1024)} %bitcast.161, f32[4096,16]{1,0:T(8,128)} %copy.329, f32[]{:T(128)} %constant.173.clone.1), kind=kCustom, calls=%fused_computation.36 | custom fusion | flops 65536 | bytes 524800 | tf_op jit(solution)/shard_map/scatter-add | solution.py:106
  366.3 16.3 %gather_fusion.3 = f32[4096,16]{1,0:T(8,128)} fusion(f32[16,8192]{0,1:T(8,128)} %bitcast.128, s32[4096]{0:T(1024)S(1)} %broadcast_clamp_fusion), kind=kCustom, calls=%fused_computation.3 | custom fusion | bytes 540672 | tf_op jit(solution)/shard_map/gather | solution.py:90
  386.0 11.4 %all-to-all-start.3 = ((f32[128,1,512]{2,1,0:T(1,128)}), f32[128,1,512]{2,1,0:T(1,128)}, u32[]{:S(2)}, u32[]{:S(2)}) async-start(f32[128,1,512]{2,1,0:T(1,128)} %reshape.323), calls=%async_computation.3 | async-start | bytes 524288 | tf_op jit(solution)/shard_map/all_to_all | solution.py:89
  423.0 24.9 %scatter_custom_fusion.4 = f32[16,8192]{0,1:T(8,128)} fusion(s32[4096]{0:T(1024)} %bitcast.162, f32[4096,16]{1,0:T(8,128)} %copy.344, f32[]{:T(128)} %constant.173.clone.1), kind=kCustom, calls=%fused_computation.34 | custom fusion | flops 65536 | bytes 524800 | tf_op jit(solution)/shard_map/scatter-add | solution.py:106
  473.1 16.3 %gather_fusion.4 = f32[4096,16]{1,0:T(8,128)} fusion(f32[16,8192]{0,1:T(8,128)} %bitcast.129, s32[4096]{0:T(1024)S(1)} %broadcast_clamp_fusion), kind=kCustom, calls=%fused_computation.4 | custom fusion | bytes 540672 | tf_op jit(solution)/shard_map/gather | solution.py:90
  532.5 24.9 %scatter_custom_fusion.5 = f32[16,8192]{0,1:T(8,128)} fusion(s32[4096]{0:T(1024)} %bitcast.163, f32[4096,16]{1,0:T(8,128)} %copy.359, f32[]{:T(128)} %constant.173.clone.1), kind=kCustom, calls=%fused_computation.32 | custom fusion | flops 65536 | bytes 524800 | tf_op jit(solution)/shard_map/scatter-add | solution.py:106
  582.1 16.3 %gather_fusion.5 = f32[4096,16]{1,0:T(8,128)} fusion(f32[16,8192]{0,1:T(8,128)} %bitcast.130, s32[4096]{0:T(1024)S(1)} %broadcast_clamp_fusion), kind=kCustom, calls=%fused_computation.5 | custom fusion | bytes 540672 | tf_op jit(solution)/shard_map/gather | solution.py:90
  639.4 24.9 %scatter_custom_fusion.6 = f32[16,8192]{0,1:T(8,128)} fusion(s32[4096]{0:T(1024)} %bitcast.164, f32[4096,16]{1,0:T(8,128)} %copy.374, f32[]{:T(128)} %constant.173.clone.1), kind=kCustom, calls=%fused_computation.30 | custom fusion | flops 65536 | bytes 524800 | tf_op jit(solution)/shard_map/scatter-add | solution.py:106
  690.4 16.3 %gather_fusion.6 = f32[4096,16]{1,0:T(8,128)} fusion(f32[16,8192]{0,1:T(8,128)} %bitcast.124, s32[4096]{0:T(1024)S(1)} %broadcast_clamp_fusion), kind=kCustom, calls=%fused_computation.6 | custom fusion | bytes 540672 | tf_op jit(solution)/shard_map/gather | solution.py:90
  712.3 11.4 %all-to-all-start.6 = ((f32[128,1,512]{2,1,0:T(1,128)}), f32[128,1,512]{2,1,0:T(1,128)}, u32[]{:S(2)}, u32[]{:S(2)}) async-start(f32[128,1,512]{2,1,0:T(1,128)} %reshape.329), calls=%async_computation.6 | async-start | bytes 524288 | tf_op jit(solution)/shard_map/all_to_all | solution.py:89
  760.6 24.9 %scatter_custom_fusion.7 = f32[16,8192]{0,1:T(8,128)} fusion(s32[4096]{0:T(1024)} %bitcast.165, f32[4096,16]{1,0:T(8,128)} %copy.389, f32[]{:T(128)} %constant.173.clone.1), kind=kCustom, calls=%fused_computation.28 | custom fusion | flops 65536 | bytes 524800 | tf_op jit(solution)/shard_map/scatter-add | solution.py:106
  795.3 22.7 %psum.35 = f32[256,16]{0,1:T(8,128)S(1)} all-reduce(f32[256,16]{0,1:T(8,128)S(1)} %fusion.24), channel_id=1, replica_groups=mesh['gx'=8,'gy'=4,'gz'=4] {'gx'}, use_global_device_ids=true, to_apply=%region_9.10 | all-reduce | flops 4096 | bytes 32768 | tf_op jit(solution)/shard_map/psum | solution.py:129
  818.0 61.3 %psum.36 = f32[256,16]{0,1:T(8,128)S(1)} all-reduce(f32[256,16]{0,1:T(8,128)S(1)} %psum.35), channel_id=1, replica_groups=mesh['gx'=8,'gy'=4,'gz'=4] {'gy','gz'}, use_global_device_ids=true, to_apply=%region_10.11 | all-reduce | flops 4096 | bytes 32768 | tf_op jit(solution)/shard_map/psum | solution.py:130
  886.5 78.9 %psum.37 = f32[256,16]{0,1:T(8,128)S(1)} all-reduce(f32[256,16]{0,1:T(8,128)S(1)} %fusion.27), channel_id=1, replica_groups=mesh['gx'=8,'gy'=4,'gz'=4] {'gx','gy','gz'}, use_global_device_ids=true, to_apply=%region_11.12 | all-reduce | flops 4096 | bytes 32768 | tf_op jit(solution)/shard_map/psum | solution.py:137
  976.8 62.8 %all-reduce = (f32[16,16]{0,1:T(8,128)S(1)}, f32[16,64]{0,1:T(8,128)S(1)}) all-reduce(f32[16,16]{0,1:T(8,128)S(1)} %fusion.165, f32[16,64]{0,1:T(8,128)S(1)} %select_bitcast_fusion), channel_id=1, replica_groups=mesh['gx'=8,'gy'=4,'gz'=4] {'gx','gy','gz'}, use_global_device_ids=true, to_apply=%region_12.13 | all-reduce | flops 1280 | bytes 10240 | tf_op jit(solution)/shard_map/psum | solution.py:142
  (387 shorter events, 450.6 us)
Async XLA Ops:
  1.6 39.6 %collective-permute-start = (f32[1,16,128]{2,1,0:T(8,128)S(1)}, f32[1,16,128]{2,1,0:T(8,128)S(1)}, u32[]{:S(2)}, u32[]{:S(2)}) collective-permute-start(f32[1,16,128]{2,1,0:T(8,128)S(1)} %slice.432), channel_id=1, source_target_pairs={{0,16},{16,32},{32,48},{48,64},{64,80},{80,96},{96,112},{1,17},{17... | collective-permute-start | bytes 24584 | tf_op jit(solution)/shard_map/ppermute | solution.py:13
  6.9 34.3 %collective-permute-start.1 = (f32[4,1,128]{2,1,0:T(1,128)S(1)}, f32[4,1,128]{2,1,0:T(1,128)S(1)}, u32[]{:S(2)}, u32[]{:S(2)}) collective-permute-start(f32[4,1,128]{2,1,0:T(1,128)S(1)} %slice.434), channel_id=1, source_target_pairs={{0,4},{4,8},{8,12},{1,5},{5,9},{9,13},{2,6},{6,10},{10,14},{3,7},{... | collective-permute-start | bytes 6152 | tf_op jit(solution)/shard_map/ppermute | solution.py:13
  11.0 30.2 %collective-permute-start.2 = (f32[4,16,1]{2,1,0:T(8,128)S(1)}, f32[4,16,1]{2,1,0:T(8,128)S(1)}, u32[]{:S(2)}, u32[]{:S(2)}) collective-permute-start(f32[4,16,1]{2,1,0:T(8,128)S(1)} %slice.436), channel_id=1, source_target_pairs={{0,1},{1,2},{2,3},{4,5},{5,6},{6,7},{8,9},{9,10},{10,11},{12,13},{... | collective-permute-start | bytes 776 | tf_op jit(solution)/shard_map/ppermute | solution.py:13
  51.0 38.8 %collective-permute-start.5 = (f32[16,6,1,128]{3,0,2,1:T(8,128)S(1)}, f32[16,6,1,128]{3,0,2,1:T(8,128)S(1)}, u32[]{:S(2)}, u32[]{:S(2)}) collective-permute-start(f32[16,6,1,128]{3,0,2,1:T(8,128)S(1)} %copy.398), channel_id=1, source_target_pairs={{4,0},{8,4},{12,8},{5,1},{9,5},{13,9},{6,2},{10,6},{14,10},{7,3},{... | collective-permute-start | bytes 147464 | tf_op jit(solution)/shard_map/ppermute | solution.py:24
  52.3 37.6 %collective-permute-start.6 = (f32[16,6,1,128]{3,0,2,1:T(8,128)S(1)}, f32[16,6,1,128]{3,0,2,1:T(8,128)S(1)}, u32[]{:S(2)}, u32[]{:S(2)}) collective-permute-start(f32[16,6,1,128]{3,0,2,1:T(8,128)S(1)} %copy.399), channel_id=1, source_target_pairs={{0,4},{4,8},{8,12},{1,5},{5,9},{9,13},{2,6},{6,10},{10,14},{3,7},{... | collective-permute-start | bytes 147464 | tf_op jit(solution)/shard_map/ppermute | solution.py:23
  78.7 23.4 %all-to-all-start = ((f32[128,1,512]{2,1,0:T(1,128)}), f32[128,1,512]{2,1,0:T(1,128)S(1)}, u32[]{:S(2)}, u32[]{:S(2)}) async-start(f32[128,1,512]{2,1,0:T(1,128)} %reshape.317), calls=%async_computation | async-start | bytes 524288 | tf_op jit(solution)/shard_map/all_to_all | solution.py:89
  153.2 39.1 %collective-permute-start.11 = (f32[16,6,1,128]{3,0,2,1:T(8,128)S(1)}, f32[16,6,1,128]{3,0,2,1:T(8,128)S(1)}, u32[]{:S(2)}, u32[]{:S(2)}) collective-permute-start(f32[16,6,1,128]{3,0,2,1:T(8,128)S(1)} %copy.400), channel_id=1, source_target_pairs={{4,0},{8,4},{12,8},{5,1},{9,5},{13,9},{6,2},{10,6},{14,10},{7,3},{... | collective-permute-start | bytes 147464 | tf_op jit(solution)/shard_map/ppermute | solution.py:24
  154.5 37.9 %collective-permute-start.12 = (f32[16,6,1,128]{3,0,2,1:T(8,128)S(1)}, f32[16,6,1,128]{3,0,2,1:T(8,128)S(1)}, u32[]{:S(2)}, u32[]{:S(2)}) collective-permute-start(f32[16,6,1,128]{3,0,2,1:T(8,128)S(1)} %copy.401), channel_id=1, source_target_pairs={{0,4},{4,8},{8,12},{1,5},{5,9},{9,13},{2,6},{6,10},{10,14},{3,7},{... | collective-permute-start | bytes 147464 | tf_op jit(solution)/shard_map/ppermute | solution.py:23
  180.9 23.6 %all-to-all-start.1 = ((f32[128,1,512]{2,1,0:T(1,128)}), f32[128,1,512]{2,1,0:T(1,128)}, u32[]{:S(2)}, u32[]{:S(2)}) async-start(f32[128,1,512]{2,1,0:T(1,128)} %reshape.319), calls=%async_computation.1 | async-start | bytes 524288 | tf_op jit(solution)/shard_map/all_to_all | solution.py:89
  255.9 39.3 %collective-permute-start.17 = (f32[16,6,1,128]{3,0,2,1:T(8,128)S(1)}, f32[16,6,1,128]{3,0,2,1:T(8,128)S(1)}, u32[]{:S(2)}, u32[]{:S(2)}) collective-permute-start(f32[16,6,1,128]{3,0,2,1:T(8,128)S(1)} %copy.402), channel_id=1, source_target_pairs={{4,0},{8,4},{12,8},{5,1},{9,5},{13,9},{6,2},{10,6},{14,10},{7,3},{... | collective-permute-start | bytes 147464 | tf_op jit(solution)/shard_map/ppermute | solution.py:24
  257.5 37.9 %collective-permute-start.18 = (f32[16,6,1,128]{3,0,2,1:T(8,128)S(1)}, f32[16,6,1,128]{3,0,2,1:T(8,128)S(1)}, u32[]{:S(2)}, u32[]{:S(2)}) collective-permute-start(f32[16,6,1,128]{3,0,2,1:T(8,128)S(1)} %copy.403), channel_id=1, source_target_pairs={{0,4},{4,8},{8,12},{1,5},{5,9},{9,13},{2,6},{6,10},{10,14},{3,7},{... | collective-permute-start | bytes 147464 | tf_op jit(solution)/shard_map/ppermute | solution.py:23
  283.8 25.2 %all-to-all-start.2 = ((f32[128,1,512]{2,1,0:T(1,128)}), f32[128,1,512]{2,1,0:T(1,128)}, u32[]{:S(2)}, u32[]{:S(2)}) async-start(f32[128,1,512]{2,1,0:T(1,128)} %reshape.321), calls=%async_computation.2 | async-start | bytes 524288 | tf_op jit(solution)/shard_map/all_to_all | solution.py:89
  358.4 39.1 %collective-permute-start.23 = (f32[16,6,1,128]{3,0,2,1:T(8,128)S(1)}, f32[16,6,1,128]{3,0,2,1:T(8,128)S(1)}, u32[]{:S(2)}, u32[]{:S(2)}) collective-permute-start(f32[16,6,1,128]{3,0,2,1:T(8,128)S(1)} %copy.404), channel_id=1, source_target_pairs={{4,0},{8,4},{12,8},{5,1},{9,5},{13,9},{6,2},{10,6},{14,10},{7,3},{... | collective-permute-start | bytes 147464 | tf_op jit(solution)/shard_map/ppermute | solution.py:24
  359.7 37.8 %collective-permute-start.24 = (f32[16,6,1,128]{3,0,2,1:T(8,128)S(1)}, f32[16,6,1,128]{3,0,2,1:T(8,128)S(1)}, u32[]{:S(2)}, u32[]{:S(2)}) collective-permute-start(f32[16,6,1,128]{3,0,2,1:T(8,128)S(1)} %copy.405), channel_id=1, source_target_pairs={{0,4},{4,8},{8,12},{1,5},{5,9},{9,13},{2,6},{6,10},{10,14},{3,7},{... | collective-permute-start | bytes 147464 | tf_op jit(solution)/shard_map/ppermute | solution.py:23
  386.0 27.2 %all-to-all-start.3 = ((f32[128,1,512]{2,1,0:T(1,128)}), f32[128,1,512]{2,1,0:T(1,128)}, u32[]{:S(2)}, u32[]{:S(2)}) async-start(f32[128,1,512]{2,1,0:T(1,128)} %reshape.323), calls=%async_computation.3 | async-start | bytes 524288 | tf_op jit(solution)/shard_map/all_to_all | solution.py:89
  464.0 39.6 %collective-permute-start.29 = (f32[16,6,1,128]{3,0,2,1:T(8,128)}, f32[16,6,1,128]{3,0,2,1:T(8,128)}, u32[]{:S(2)}, u32[]{:S(2)}) collective-permute-start(f32[16,6,1,128]{3,0,2,1:T(8,128)} %copy.406), channel_id=1, source_target_pairs={{4,0},{8,4},{12,8},{5,1},{9,5},{13,9},{6,2},{10,6},{14,10},{7,3},{... | collective-permute-start | bytes 147464 | tf_op jit(solution)/shard_map/ppermute | solution.py:24
  465.9 38.6 %collective-permute-start.30 = (f32[16,6,1,128]{3,0,2,1:T(8,128)}, f32[16,6,1,128]{3,0,2,1:T(8,128)}, u32[]{:S(2)}, u32[]{:S(2)}) collective-permute-start(f32[16,6,1,128]{3,0,2,1:T(8,128)} %copy.407), channel_id=1, source_target_pairs={{0,4},{4,8},{8,12},{1,5},{5,9},{9,13},{2,6},{6,10},{10,14},{3,7},{... | collective-permute-start | bytes 147464 | tf_op jit(solution)/shard_map/ppermute | solution.py:23
  492.8 30.5 %all-to-all-start.4 = ((f32[128,1,512]{2,1,0:T(1,128)}), f32[128,1,512]{2,1,0:T(1,128)}, u32[]{:S(2)}, u32[]{:S(2)}) async-start(f32[128,1,512]{2,1,0:T(1,128)} %reshape.325), calls=%async_computation.4 | async-start | bytes 524288 | tf_op jit(solution)/shard_map/all_to_all | solution.py:89
  572.9 40.8 %collective-permute-start.35 = (f32[16,6,1,128]{3,0,2,1:T(8,128)}, f32[16,6,1,128]{3,0,2,1:T(8,128)S(1)}, u32[]{:S(2)}, u32[]{:S(2)}) collective-permute-start(f32[16,6,1,128]{3,0,2,1:T(8,128)} %copy.408), channel_id=1, source_target_pairs={{4,0},{8,4},{12,8},{5,1},{9,5},{13,9},{6,2},{10,6},{14,10},{7,3},{... | collective-permute-start | bytes 147464 | tf_op jit(solution)/shard_map/ppermute | solution.py:24
  574.8 39.0 %collective-permute-start.36 = (f32[16,6,1,128]{3,0,2,1:T(8,128)}, f32[16,6,1,128]{3,0,2,1:T(8,128)}, u32[]{:S(2)}, u32[]{:S(2)}) collective-permute-start(f32[16,6,1,128]{3,0,2,1:T(8,128)} %copy.409), channel_id=1, source_target_pairs={{0,4},{4,8},{8,12},{1,5},{5,9},{9,13},{2,6},{6,10},{10,14},{3,7},{... | collective-permute-start | bytes 147464 | tf_op jit(solution)/shard_map/ppermute | solution.py:23
  604.0 26.6 %all-to-all-start.5 = ((f32[128,1,512]{2,1,0:T(1,128)}), f32[128,1,512]{2,1,0:T(1,128)S(1)}, u32[]{:S(2)}, u32[]{:S(2)}) async-start(f32[128,1,512]{2,1,0:T(1,128)} %reshape.327), calls=%async_computation.5 | async-start | bytes 524288 | tf_op jit(solution)/shard_map/all_to_all | solution.py:89
  681.2 42.5 %collective-permute-start.41 = (f32[16,6,1,128]{3,0,2,1:T(8,128)}, f32[16,6,1,128]{3,0,2,1:T(8,128)}, u32[]{:S(2)}, u32[]{:S(2)}) collective-permute-start(f32[16,6,1,128]{3,0,2,1:T(8,128)} %copy.410), channel_id=1, source_target_pairs={{4,0},{8,4},{12,8},{5,1},{9,5},{13,9},{6,2},{10,6},{14,10},{7,3},{... | collective-permute-start | bytes 147464 | tf_op jit(solution)/shard_map/ppermute | solution.py:24
  683.1 41.5 %collective-permute-start.42 = (f32[16,6,1,128]{3,0,2,1:T(8,128)}, f32[16,6,1,128]{3,0,2,1:T(8,128)}, u32[]{:S(2)}, u32[]{:S(2)}) collective-permute-start(f32[16,6,1,128]{3,0,2,1:T(8,128)} %copy.411), channel_id=1, source_target_pairs={{0,4},{4,8},{8,12},{1,5},{5,9},{9,13},{2,6},{6,10},{10,14},{3,7},{... | collective-permute-start | bytes 147464 | tf_op jit(solution)/shard_map/ppermute | solution.py:23
  712.3 33.5 %all-to-all-start.6 = ((f32[128,1,512]{2,1,0:T(1,128)}), f32[128,1,512]{2,1,0:T(1,128)}, u32[]{:S(2)}, u32[]{:S(2)}) async-start(f32[128,1,512]{2,1,0:T(1,128)} %reshape.329), calls=%async_computation.6 | async-start | bytes 524288 | tf_op jit(solution)/shard_map/all_to_all | solution.py:89
  (69 other events, 907.4 us)
